TPU v7x, 128 devices: a whole 4x4x4 slice. The times are simulated.
128 devices in a mesh: replica: 8 (over z_hi, y), tensor: 16 (over x, z_lo, core).
Axes of the slice: x: 4, y: 4, z: 4 (z_hi: 2, z_lo: 2; z = z_hi * 2 + z_lo), core: 2. Of those that a mesh axis runs over, the one named last changes fastest.
Arguments:
- queries: bfloat16 [1024, 8192], P('replica', 'tensor'), may hold values from -200 to 200
- new_kv: bfloat16 [1024, 1024], P('replica'), may hold values from -8 to 8
- kv_pool: bfloat16 [1024, 64, 1024], P(('replica', 'tensor')), may hold values from -6 to 6
- anchor: int32 [8, 8], replicated, may hold values from 0 to 7, as said below
- page_table: int32 [64, 16], replicated, may hold values from 0 to 7, as said below
- prefix_len: int32 [64], replicated, may hold values from 1 to 1024, 32768 in all
- turn_rows: int32 [8, 8], replicated, may hold values from 1 to 32, 128 in all within a row
- out_weight: bfloat16 [8192, 16384], P('tensor', 'replica'), may hold values from -0.5 to 0.5
- residual: bfloat16 [1024, 16384], P(None, 'replica'), may hold values from -400 to 400
- norm_gain: bfloat16 [16384], P('replica'), may hold values from 0.099609375 to 1.8984375
- gate_up: bfloat16 [16384, 2, 26624], P('replica', None, 'tensor'), may hold values from -0.046875 to 0.046875
Outputs:
- hidden: bfloat16 [1024, 26624], P('replica', 'tensor')
Inputs may be any that keep to these rules, and one draw needn't show every extreme that they name: Slot j of new replica d holds session anchor[d, j] of old replica j; for each old replica, the 8 slots that come from it name each of its 8 sessions exactly once. `page_table`: row o * 8 + s lists the pages of session s of old replica o: entry k is a local page index on device k of that replica's 16 tensor devices, whose pages are numbered (o * 16 + k) * 8 + index in kv_pool; on each device the 8 sessions use distinct pages. `prefix_len`: indexed by d * 8 + j for slot j of new replica d. `turn_rows`: each replica's entries sum to 128.
All inputs are finite; a program needn't handle non-finite values.
Results may differ from a plain program's by a relative error of at most 0.0064.
Values may be sent and summed in bfloat16 or wider, within the bound.
A program may use at most 128 MiB of HBM per device.

v0:
```python
import jax
import jax.numpy as jnp
import numpy as np
from jax import lax
from jax.sharding import PartitionSpec as P

D = 16384
HD = 128
HEADS = 64
KVH = 4
PAGE = 64
SHARE = 1
ROWS = 128
GROUP = 16
EPSILON = 1e-05


def per_device(
    queries,
    new_kv,
    kv_pool,
    anchor,
    page_table,
    prefix_len,
    turn_rows,
    out_weight,
    residual,
    norm_gain,
    gate_up,
):
    replicas = lax.axis_size("replica")
    tensors = lax.axis_size("tensor")
    replica_idx = lax.axis_index("replica")
    tensor_idx = lax.axis_index("tensor")
    sessions = SHARE * replicas
    heads_local = HEADS // tensors
    pair_width = 2 * HD
    cached_len = tensors * PAGE
    owner_head = np.arange(tensors) * heads_local // GROUP
    from_here = lax.dynamic_slice_in_dim(anchor, replica_idx * SHARE, SHARE, 1)
    table_rows = lax.dynamic_slice_in_dim(page_table, replica_idx * sessions, sessions, 0)
    my_column = lax.dynamic_slice_in_dim(table_rows, tensor_idx, 1, 1)[:, 0]
    page_index = jnp.take(my_column, from_here.reshape(-1), axis=0)
    chosen = jnp.take(kv_pool, page_index, axis=0).reshape(replicas, SHARE, PAGE, KVH, pair_width)
    outgoing = jnp.take(chosen, owner_head, axis=3)
    outgoing = jnp.transpose(outgoing, (0, 3, 1, 2, 4)).reshape(
        replicas * tensors, SHARE, PAGE, pair_width
    )
    arrived = lax.all_to_all(
        outgoing, ("replica", "tensor"), split_axis=0, concat_axis=0, tiled=True
    )
    arrived = arrived.reshape(replicas, tensors, SHARE, PAGE, pair_width)
    prefix_blocks = jnp.transpose(arrived, (0, 2, 1, 3, 4)).reshape(
        sessions, cached_len, pair_width
    )
    kv_group = tensor_idx * heads_local // GROUP
    fresh_pair = lax.dynamic_slice_in_dim(new_kv, kv_group * pair_width, pair_width, 1)
    rows_here = queries.shape[0]
    slot_rows = ROWS // 4
    query_heads = queries.reshape(rows_here, heads_local, HD)
    counts = lax.dynamic_slice_in_dim(turn_rows, replica_idx, 1, 0)[0]
    bounds = jnp.cumsum(counts, dtype=jnp.int32)
    starts = bounds - counts
    row_ids = jnp.arange(rows_here, dtype=jnp.int32)
    row_slot = jnp.sum(
        (row_ids[:, None] >= bounds[None, :]).astype(jnp.int32), axis=1, dtype=jnp.int32
    )
    offsets = jnp.arange(slot_rows, dtype=jnp.int32)
    padded_index = jnp.minimum(starts[:, None] + offsets[None, :], rows_here - 1).reshape(-1)
    slot_queries = jnp.take(query_heads, padded_index, axis=0).reshape(
        sessions, slot_rows, heads_local, HD
    )
    slot_fresh = jnp.take(fresh_pair, padded_index, axis=0).reshape(sessions, slot_rows, pair_width)
    lengths = lax.dynamic_slice_in_dim(prefix_len, replica_idx * sessions, sessions, 0)
    key_pos = jnp.arange(cached_len, dtype=jnp.int32)
    prefix_mask = (key_pos[None, :] < lengths[:, None])[:, None, :]
    fresh_mask = (offsets[None, None, :] <= offsets[None, :, None]) & (
        offsets[None, None, :] < counts[:, None, None]
    )
    score_scale = HD ** (-0.5)
    prefix_scores = (
        jnp.einsum(
            "smhd,skd->hsmk",
            slot_queries,
            prefix_blocks[:, :, :HD],
            preferred_element_type=jnp.float32,
        )
        * score_scale
    )
    fresh_scores = (
        jnp.einsum(
            "smhd,snd->hsmn",
            slot_queries,
            slot_fresh[:, :, :HD],
            preferred_element_type=jnp.float32,
        )
        * score_scale
    )
    prefix_scores = jnp.where(prefix_mask[None], prefix_scores, -jnp.inf)
    fresh_scores = jnp.where(fresh_mask[None], fresh_scores, -jnp.inf)
    row_peak = jnp.maximum(jnp.max(prefix_scores, axis=3), jnp.max(fresh_scores, axis=3))
    prefix_weights = jnp.exp(prefix_scores - row_peak[..., None])
    fresh_weights = jnp.exp(fresh_scores - row_peak[..., None])
    denominator = jnp.sum(prefix_weights, axis=3) + jnp.sum(fresh_weights, axis=3)
    mixed_values = jnp.einsum(
        "hsmk,skd->smhd",
        prefix_weights.astype(jnp.bfloat16),
        prefix_blocks[:, :, HD:],
        preferred_element_type=jnp.float32,
    )
    mixed_values = mixed_values + jnp.einsum(
        "hsmn,snd->smhd",
        fresh_weights.astype(jnp.bfloat16),
        slot_fresh[:, :, HD:],
        preferred_element_type=jnp.float32,
    )
    slot_attended = (mixed_values / jnp.transpose(denominator, (1, 2, 0))[..., None]).astype(
        jnp.bfloat16
    )
    slot_attended = slot_attended.reshape(sessions * slot_rows, heads_local * HD)
    back_index = row_slot * slot_rows + row_ids - jnp.take(starts, row_slot, axis=0)
    attended = jnp.take(slot_attended, back_index, axis=0)
    partial_out = jnp.dot(
        lax.all_gather(attended, "replica", axis=0, tiled=True),
        out_weight,
        preferred_element_type=jnp.float32,
    )
    weights_local = gate_up.reshape(gate_up.shape[0], 2 * gate_up.shape[2])
    gain_row = norm_gain.astype(jnp.float32)
    carried = residual.astype(jnp.float32) + lax.psum(partial_out, "tensor")
    squares = lax.psum(jnp.sum(carried * carried, axis=1), "replica")
    normed = (carried * lax.rsqrt(squares / D + EPSILON)[:, None] * gain_row[None, :]).astype(
        jnp.bfloat16
    )
    summed = lax.psum_scatter(
        jnp.dot(normed, weights_local, preferred_element_type=jnp.float32),
        "replica",
        scatter_dimension=0,
        tiled=True,
    )
    paired = summed.reshape(rows_here, 2, gate_up.shape[2])
    return (jax.nn.silu(paired[:, 0, :]) * paired[:, 1, :]).astype(jnp.bfloat16)


def solution(mesh):
    placed = (
        P("replica", "tensor"),
        P("replica", None),
        P(("replica", "tensor"), None, None),
        P(),
        P(),
        P(),
        P(),
        P("tensor", "replica"),
        P(None, "replica"),
        P("replica"),
        P("replica", None, "tensor"),
    )
    return jax.shard_map(
        per_device, mesh=mesh, in_specs=placed, out_specs=P("replica", "tensor"), check_vma=False
    )
```

profile of v0, /device:TPU:0, one launch (start us, length us, event | category | flops | bytes accessed | tf_op | source)
XLA Modules:
  0.0 568.3 jit_solution(5678871009920733186)
XLA Ops:
  6.5 0.0 copy-start
  6.5 0.9 constant_dynamic-slice_fusion
  7.4 0.1 copy.62
  7.6 0.8 dynamic-slice_bitcast_fusion
  8.3 0.6 gather_fusion
  9.0 0.7 pad_clamp_fusion.2
  9.7 1.8 gather_fusion.1
  11.5 1.6 gather.42
  13.1 1.4 fusion.18
  14.5 2.8 gather_fusion.2
  17.3 4.7 copy.48
  22.0 0.0 copy-start.4
  22.0 0.0 copy-start.2
  22.0 11.7 %all-to-all-start = ((bf16[128,1,64,256]{3,2,1,0:T(8,128)(2,1)}), bf16[128,1,64,256]{3,2,1,0:T(8,128)(2,1)}, u32[]{:S(2)}, u32[]{:S(2)}) async-start(bf16[128,1,64,256]{3,2,1,0:T(8,128)(2,1)} %bitcast.135), calls=%async_computation | async-start | bytes 8388608 | tf_op jit(solution)/shard_map/all_to_all | solution.py:49
  33.7 0.0 all-gather.2.cloned.1.call-start
  33.8 0.0 copy-done.4
  33.8 0.1 dynamic_slice.19
  33.9 0.7 fusion.33
  34.5 0.2 reduce-window.7
  34.7 0.7 bitcast_subtract_fusion.1
  35.4 0.1 add_minimum_fusion
  35.5 0.1 min.22
  35.6 0.0 copy-done.2
  35.7 0.9 constant_dynamic-slice_fusion.1
  36.5 1.1 gather_fusion.4
  37.7 1.0 gather_fusion.3
  38.7 0.7 fusion.39
  39.4 0.1 convert_reduce_fusion
  39.5 4.9 compare_and_fusion.1
  44.4 0.1 compare_and_fusion
  44.4 0.1 iota_compare_fusion.2
  44.5 0.1 iota_compare_fusion
  44.6 0.1 broadcast_and_fusion
  44.7 0.1 broadcast_select_fusion.2
  44.8 0.6 fusion.40
  45.4 40.4 %all-to-all-done = bf16[128,1,64,256]{3,2,1,0:T(8,128)(2,1)} async-done(((bf16[128,1,64,256]{3,2,1,0:T(8,128)(2,1)}), bf16[128,1,64,256]{3,2,1,0:T(8,128)(2,1)}, u32[]{:S(2)}, u32[]{:S(2)}) %all-to-all-start) | async-done | bytes 4194336 | tf_op jit(solution)/shard_map/all_to_all | solution.py:49
  85.8 2.4 bitcast_reduce_fusion
  88.3 2.7 fusion.6
  91.0 1.0 fusion.4
  92.0 0.1 fusion.21
  92.2 0.3 fusion.17
  92.5 0.1 copy.54
  92.7 0.8 gather_fusion.5
  93.5 0.7 broadcast_select_fusion.1
  94.3 0.0 all-gather.2.cloned.1.call-update
  94.3 0.0 all-reduce.2.cloned.1.call-start
  94.4 47.4 %all-gather.2.cloned.1.call-done = bf16[1024,512]{1,0:T(8,128)(2,1)} async-done(((bf16[128,512]{1,0:T(8,128)(2,1)}), bf16[1024,512]{1,0:T(8,128)(2,1)}) %all-gather.2.cloned.1.call-update) | async-done | bytes 1048592 | tf_op jit(solution)/shard_map/all_gather | solution.py:124
  141.7 0.0 copy-done
  141.7 6.8 %fusion.41 = f32[1024,2048]{1,0:T(8,128)} fusion(bf16[1024,512]{1,0:T(8,128)(2,1)} %all-gather.2.cloned.1.call-done, bf16[512,2048]{1,0:T(8,128)(2,1)S(1)} %copy-done), kind=kOutput, calls=%fused_computation.105 | convolution fusion | flops 2147483648 | bytes 11534336 | tf_op jit(solution)/shard_map/dot_general | solution.py:123
  148.5 0.0 all-reduce.2.cloned.1.call-update
  148.6 0.0 reduce-scatter.2.cloned.1.call-start
  148.6 0.6 copy-done.3
  149.2 14.3 %copy.66 = bf16[256,8,2,1664]{3,1,2,0:T(8,128)(2,1)} copy(bf16[256,8,2,1664]{3,2,1,0:T(2,128)(2,1)} %bitcast.137) | data formatting | bytes 27262976
  163.5 177.2 %all-reduce.2.cloned.1.call-done = f32[1024,2048]{1,0:T(8,128)} async-done(((f32[1024,2048]{1,0:T(8,128)}), f32[1024,2048]{1,0:T(8,128)}) %all-reduce.2.cloned.1.call-update) | async-done | bytes 8388624 | tf_op jit(solution)/shard_map/psum | solution.py:130
  340.7 5.7 %multiply_reduce_fusion = f32[1024]{0:T(1024)S(1)} fusion(f32[1024,2048]{1,0:T(8,128)} %all-reduce.2.cloned.1.call-done, bf16[1024,2048]{1,0:T(8,128)(2,1)} %param.20), kind=kLoop, calls=%fused_computation.7 | loop fusion | flops 8387584 | bytes 12587008 | tf_op jit(solution)/shard_map/reduce_sum | solution.py:131
  346.4 23.9 %psum.15 = f32[1024]{0:T(1024)S(1)} all-reduce(f32[1024]{0:T(1024)S(1)} %multiply_reduce_fusion), channel_id=1, replica_groups=mesh['replica'=8,'tensor'=16] {'replica'}, use_global_device_ids=true, to_apply=%region_8.9 | all-reduce | flops 1024 | bytes 8192 | tf_op jit(solution)/shard_map/psum | solution.py:131
  370.3 24.2 %fusion = f32[1024,3328]{1,0:T(8,128)} fusion(bf16[2048,3328]{1,0:T(8,128)(2,1)} %bitcast.138, f32[1024,2048]{1,0:T(8,128)} %all-reduce.2.cloned.1.call-done, bf16[1024,2048]{1,0:T(8,128)(2,1)} %param.20, f32[2048]{0:T(1024)S(1)} %convert_element_type.29, f32[1024]{0:T(1024)S(1)} %add_rsqrt_fusion), kind=kOutput, calls=%fused_computation.9 | convolution fusion | flops 13969129472 | bytes 39858176 | tf_op jit(solution)/shard_map/dot_general | solution.py:136
  394.5 0.0 reduce-scatter.2.cloned.1.call-update
  394.6 0.0 copy-start.1
  394.6 159.6 %reduce-scatter.2.cloned.1.call-done = f32[128,3328]{1,0:T(8,128)} async-done(((f32[1024,3328]{1,0:T(8,128)}), f32[128,3328]{1,0:T(8,128)}) %reduce-scatter.2.cloned.1.call-update) | async-done | bytes 1703952 | tf_op jit(solution)/shard_map/reduce_scatter | solution.py:135
  554.2 3.1 reshape.267
  557.3 3.4 fusion.38
  560.7 1.0 fusion.20
  561.7 0.0 copy-done.1
  (17 shorter events, 0.2 us)
Async XLA Ops:
  6.5 135.2 %copy-start = (bf16[512,2048]{1,0:T(8,128)(2,1)S(1)}, bf16[512,2048]{1,0:T(8,128)(2,1)}, u32[]{:S(2)}) copy-start(bf16[512,2048]{1,0:T(8,128)(2,1)} %param.19) | copy-start | bytes 6291460
  22.0 11.8 %copy-start.4 = (s32[64]{0:T(128)S(1)}, s32[64]{0:T(128)}, u32[]{:S(2)}) copy-start(s32[64]{0:T(128)} %param.17) | copy-start | bytes 772
  22.0 13.6 %copy-start.2 = (bf16[128,512]{1,0:T(8,128)(2,1)S(1)}, bf16[128,512]{1,0:T(8,128)(2,1)}, u32[]{:S(2)}) copy-start(bf16[128,512]{1,0:T(8,128)(2,1)} %param.12) | copy-start | bytes 393220
  22.0 63.9 %all-to-all-start = ((bf16[128,1,64,256]{3,2,1,0:T(8,128)(2,1)}), bf16[128,1,64,256]{3,2,1,0:T(8,128)(2,1)}, u32[]{:S(2)}, u32[]{:S(2)}) async-start(bf16[128,1,64,256]{3,2,1,0:T(8,128)(2,1)} %bitcast.135), calls=%async_computation | async-start | bytes 8388608 | tf_op jit(solution)/shard_map/all_to_all | solution.py:49
  33.7 108.0 %all-gather.2.cloned.1.call-start = ((), (), s32[]{:S(2)}) async-start(), calls=%async_computation.2 | async-start | bytes 1179648 | tf_op jit(solution)/shard_map/all_gather | solution.py:124
  94.3 246.4 %all-reduce.2.cloned.1.call-start = ((), (), s32[]{:S(2)}) async-start(), calls=%async_computation.3 | async-start | bytes 16777216 | tf_op jit(solution)/shard_map/psum | solution.py:130
  148.5 0.7 copy-start.3
  148.6 405.6 %reduce-scatter.2.cloned.1.call-start = ((), (), s32[]{:S(2)}) async-start(), calls=%async_computation.4 | async-start | bytes 15335424 | tf_op jit(solution)/shard_map/reduce_scatter | solution.py:135
  394.6 167.2 %copy-start.1 = (bf16[512,2048]{1,0:T(8,128)(2,1)S(1)}, bf16[512,2048]{1,0:T(8,128)(2,1)}, u32[]{:S(2)}) copy-start(bf16[512,2048]{1,0:T(8,128)(2,1)} %param.19) | copy-start | bytes 6291460
Sparse Core Ops, SparseCore 0:
  94.4 47.2 all-gather.1
  148.7 191.9 all-reduce.1
  394.7 159.4 reduce-scatter.1
where the time goes:
time: 569 us; the launch traced here: 568 us
  waiting for transfers between devices  425 us (75%)
  local copies, waits for them, and re-layouts  40.4 us (7%)
  matrix products  37.1 us (7%)
  blocking collectives  23.9 us (4%)
  other arithmetic  17.1 us (3%)
  between operations  13.3 us (2%)
  starting transfers between devices  11.8 us (2%)
    psum x1, waiting for transfers between devices, per_device(): carried = residual.astype(jnp.float32) + lax.psum(partial_out, 'tensor')  177 us
    reduce_scatter x1, waiting for transfers between devices, per_device(): lax.psum_scatter(jnp.dot(normed, weights_local, preferred_element_type=jn...  160 us
    all_gather x1, waiting for transfers between devices, per_device(): lax.all_gather(attended, 'replica', axis=0, tiled=True)  47.4 us
    all_to_all x1, waiting for transfers between devices, per_device(): lax.all_to_all(outgoing, ('replica', 'tensor'), split_axis=0, concat_axis...  40.4 us
    dot_general x1, matrix products, per_device(): jnp.dot(normed, weights_local, preferred_element_type=jnp.float32)  24.2 us
    psum x1, blocking collectives, per_device(): squares = lax.psum(jnp.sum(carried * carried, axis=1), 'replica')  23.9 us
    unnamed x13, local copies, waits for them, and re-layouts  15 us
    all_to_all x1, starting transfers between devices, per_device(): lax.all_to_all(outgoing, ('replica', 'tensor'), split_axis=0, concat_axis...  11.7 us
  transfers between devices with their start and end apart: 4, of which 4 were waited for; matrix products, arithmetic and copies ran while one was open for 5% of the time, Pallas kernels for 0%

commit v1 on v0

--- a/solution.py
+++ b/solution.py
@@ -1,3 +1,4 @@
+import functools
 import jax
 import jax.numpy as jnp
 import numpy as np
@@ -13,6 +14,16 @@
 ROWS = 128
 GROUP = 16
 EPSILON = 1e-05
+
+
+def meet_widths(local_values, axis_name, dim_no):
+    earlier = lax.psum(1, axis_name=axis_name)
+    res = jnp.stack([local_values] * earlier, axis=0)
+    shaped = lax.all_to_all(res, axis_name=axis_name, split_axis=0, concat_axis=0)
+    return jnp.concatenate(shaped, dim_no)
+
+
+block_perform = functools.partial(meet_widths, axis_name="replica", dim_no=0)
 
 
 def per_device(
@@ -120,11 +131,7 @@
     slot_attended = slot_attended.reshape(sessions * slot_rows, heads_local * HD)
     back_index = row_slot * slot_rows + row_ids - jnp.take(starts, row_slot, axis=0)
     attended = jnp.take(slot_attended, back_index, axis=0)
-    partial_out = jnp.dot(
-        lax.all_gather(attended, "replica", axis=0, tiled=True),
-        out_weight,
-        preferred_element_type=jnp.float32,
-    )
+    partial_out = jnp.dot(block_perform(attended), out_weight, preferred_element_type=jnp.float32)
     weights_local = gate_up.reshape(gate_up.shape[0], 2 * gate_up.shape[2])
     gain_row = norm_gain.astype(jnp.float32)
     carried = residual.astype(jnp.float32) + lax.psum(partial_out, "tensor")

time: 569 us -> 540 us (0.949)
  waiting for transfers between devices: 425 us -> 378 us
  blocking collectives: 23.9 us -> 43.4 us
    all_gather x1 -> x0, waiting for transfers between devices: 47.4 us -> none  [per_device(): lax.all_gather(attended, 'replica', axis=0, tiled=True)]
    all_to_all x0 -> x1, blocking collectives: none -> 19.8 us  [meet_widths(): lax.all_to_all(res, axis_name=axis_name, split_axis=0, concat_axis=0)]
  transfers between devices with their start and end apart: 4 -> 3, of which waited for: 4 -> 3; matrix products, arithmetic and copies ran while one was open for 5% -> 5% of each run, Pallas kernels for 0% -> 0%
where the time goes in v1:
time: 540 us; the launch traced here: 539 us
  waiting for transfers between devices  378 us (70%)
  blocking collectives  43.4 us (8%)
  local copies, waits for them, and re-layouts  40.3 us (7%)
  matrix products  35.9 us (7%)
  other arithmetic  16.5 us (3%)
  between operations  13.7 us (3%)
  starting transfers between devices  12 us (2%)
    psum x1, waiting for transfers between devices, per_device(): carried = residual.astype(jnp.float32) + lax.psum(partial_out, 'tensor')  178 us
    reduce_scatter x1, waiting for transfers between devices, per_device(): lax.psum_scatter(jnp.dot(normed, weights_local, preferred_element_type=jn...  160 us
    all_to_all x1, waiting for transfers between devices, per_device(): lax.all_to_all(outgoing, ('replica', 'tensor'), split_axis=0, concat_axis...  40.4 us
    dot_general x1, matrix products, per_device(): jnp.dot(normed, weights_local, preferred_element_type=jnp.float32)  24.2 us
    psum x1, blocking collectives, per_device(): squares = lax.psum(jnp.sum(carried * carried, axis=1), 'replica')  23.7 us
    all_to_all x1, blocking collectives, meet_widths(): lax.all_to_all(res, axis_name=axis_name, split_axis=0, concat_axis=0)  19.8 us
    unnamed x13, local copies, waits for them, and re-layouts  14.8 us
    all_to_all x1, starting transfers between devices, per_device(): lax.all_to_all(outgoing, ('replica', 'tensor'), split_axis=0, concat_axis...  11.7 us
  transfers between devices with their start and end apart: 3, of which 3 were waited for; matrix products, arithmetic and copies ran while one was open for 5% of the time, Pallas kernels for 0%

profile of v1, /device:TPU:0, one launch (start us, length us, event | category | flops | bytes accessed | tf_op | source)
XLA Modules:
  0.0 539.2 jit_solution(1322887215405611842)
XLA Ops:
  6.5 0.0 copy-start
  6.5 0.9 constant_dynamic-slice_fusion
  7.4 0.1 copy.62
  7.6 0.8 dynamic-slice_bitcast_fusion
  8.3 0.6 gather_fusion
  9.0 0.7 pad_clamp_fusion.2
  9.7 1.8 gather_fusion.1
  11.5 1.6 gather.42
  13.1 1.4 fusion.18
  14.5 2.8 gather_fusion.2
  17.3 4.7 copy.48
  22.0 0.0 copy-start.4
  22.0 0.0 copy-start.2
  22.0 11.7 %all-to-all-start = ((bf16[128,1,64,256]{3,2,1,0:T(8,128)(2,1)}), bf16[128,1,64,256]{3,2,1,0:T(8,128)(2,1)}, u32[]{:S(2)}, u32[]{:S(2)}) async-start(bf16[128,1,64,256]{3,2,1,0:T(8,128)(2,1)} %bitcast.136), calls=%async_computation | async-start | bytes 8388608 | tf_op jit(solution)/shard_map/all_to_all | solution.py:60
  33.7 0.0 all-reduce.2.cloned.1.call-start
  33.8 0.0 copy-done.4
  33.8 0.1 dynamic_slice.19
  33.9 0.7 fusion.33
  34.5 0.2 reduce-window.7
  34.7 0.7 bitcast_subtract_fusion.1
  35.4 0.1 add_minimum_fusion
  35.5 0.1 min.22
  35.6 0.0 copy-done.2
  35.7 0.9 constant_dynamic-slice_fusion.1
  36.5 1.1 gather_fusion.4
  37.7 1.0 gather_fusion.3
  38.7 0.7 fusion.39
  39.4 0.1 convert_reduce_fusion
  39.5 4.9 compare_and_fusion.1
  44.4 0.1 compare_and_fusion
  44.4 0.1 iota_compare_fusion.2
  44.5 0.1 iota_compare_fusion
  44.6 0.1 broadcast_and_fusion
  44.7 0.1 broadcast_select_fusion.2
  44.8 0.6 fusion.40
  45.4 40.4 %all-to-all-done = bf16[128,1,64,256]{3,2,1,0:T(8,128)(2,1)} async-done(((bf16[128,1,64,256]{3,2,1,0:T(8,128)(2,1)}), bf16[128,1,64,256]{3,2,1,0:T(8,128)(2,1)}, u32[]{:S(2)}, u32[]{:S(2)}) %all-to-all-start) | async-done | bytes 4194336 | tf_op jit(solution)/shard_map/all_to_all | solution.py:60
  85.8 2.4 bitcast_reduce_fusion
  88.3 2.7 fusion.6
  91.0 1.0 fusion.4
  92.0 0.1 fusion.21
  92.2 0.3 fusion.17
  92.5 0.1 copy.54
  92.7 0.8 gather_fusion.5
  93.5 0.1 broadcast_select_fusion.1
  93.6 0.1 stack.2
  93.7 19.8 %all_to_all.10 = bf16[8,128,512]{2,1,0:T(8,128)(2,1)S(1)} all-to-all(bf16[8,128,512]{2,1,0:T(8,128)(2,1)S(1)} %stack.2), channel_id=1, replica_groups=mesh['replica'=8,'tensor'=16] {'replica'}, dimensions={0} | all-to-all | bytes 2097152 | tf_op jit(solution)/shard_map/all_to_all | solution.py:22
  113.5 0.0 copy-done
  113.5 5.6 %fusion.41 = f32[1024,2048]{1,0:T(8,128)} fusion(bf16[1024,512]{1,0:T(8,128)(2,1)S(1)} %bitcast.141, bf16[512,2048]{1,0:T(8,128)(2,1)S(1)} %copy-done), kind=kOutput, calls=%fused_computation.105 | convolution fusion | flops 2147483648 | bytes 11534336 | tf_op jit(solution)/shard_map/dot_general | solution.py:134
  119.1 0.0 copy-start.3
  119.1 0.0 all-reduce.2.cloned.1.call-update
  119.1 0.2 reduce-scatter.2.cloned.1.call-start
  119.3 0.4 copy-done.3
  119.8 14.3 %copy.66 = bf16[256,8,2,1664]{3,1,2,0:T(8,128)(2,1)} copy(bf16[256,8,2,1664]{3,2,1,0:T(2,128)(2,1)} %bitcast.138) | data formatting | bytes 27262976
  134.0 177.5 %all-reduce.2.cloned.1.call-done = f32[1024,2048]{1,0:T(8,128)} async-done(((f32[1024,2048]{1,0:T(8,128)}), f32[1024,2048]{1,0:T(8,128)}) %all-reduce.2.cloned.1.call-update) | async-done | bytes 8388624 | tf_op jit(solution)/shard_map/psum | solution.py:137
  311.6 5.7 %multiply_reduce_fusion = f32[1024]{0:T(1024)S(1)} fusion(f32[1024,2048]{1,0:T(8,128)} %all-reduce.2.cloned.1.call-done, bf16[1024,2048]{1,0:T(8,128)(2,1)} %param.20), kind=kLoop, calls=%fused_computation.7 | loop fusion | flops 8387584 | bytes 12587008 | tf_op jit(solution)/shard_map/reduce_sum | solution.py:138
  317.3 23.7 %psum.15 = f32[1024]{0:T(1024)S(1)} all-reduce(f32[1024]{0:T(1024)S(1)} %multiply_reduce_fusion), channel_id=1, replica_groups=mesh['replica'=8,'tensor'=16] {'replica'}, use_global_device_ids=true, to_apply=%region_8.9 | all-reduce | flops 1024 | bytes 8192 | tf_op jit(solution)/shard_map/psum | solution.py:138
  341.0 24.2 %fusion = f32[1024,3328]{1,0:T(8,128)} fusion(bf16[2048,3328]{1,0:T(8,128)(2,1)} %bitcast.139, f32[1024,2048]{1,0:T(8,128)} %all-reduce.2.cloned.1.call-done, bf16[1024,2048]{1,0:T(8,128)(2,1)} %param.20, f32[2048]{0:T(1024)S(1)} %convert_element_type.29, f32[1024]{0:T(1024)S(1)} %add_rsqrt_fusion), kind=kOutput, calls=%fused_computation.9 | convolution fusion | flops 13969129472 | bytes 39858176 | tf_op jit(solution)/shard_map/dot_general | solution.py:143
  365.2 0.0 reduce-scatter.2.cloned.1.call-update
  365.2 0.0 copy-start.1
  365.3 159.6 %reduce-scatter.2.cloned.1.call-done = f32[128,3328]{1,0:T(8,128)} async-done(((f32[1024,3328]{1,0:T(8,128)}), f32[128,3328]{1,0:T(8,128)}) %reduce-scatter.2.cloned.1.call-update) | async-done | bytes 1703952 | tf_op jit(solution)/shard_map/reduce_scatter | solution.py:142
  524.8 3.1 reshape.278
  528.0 3.4 fusion.38
  531.4 1.0 fusion.20
  532.4 0.0 copy-done.1
  (16 shorter events, 0.2 us)
Async XLA Ops:
  6.5 106.9 %copy-start = (bf16[512,2048]{1,0:T(8,128)(2,1)S(1)}, bf16[512,2048]{1,0:T(8,128)(2,1)}, u32[]{:S(2)}) copy-start(bf16[512,2048]{1,0:T(8,128)(2,1)} %param.19) | copy-start | bytes 6291460
  22.0 11.8 %copy-start.4 = (s32[64]{0:T(128)S(1)}, s32[64]{0:T(128)}, u32[]{:S(2)}) copy-start(s32[64]{0:T(128)} %param.17) | copy-start | bytes 772
  22.0 13.6 %copy-start.2 = (bf16[128,512]{1,0:T(8,128)(2,1)S(1)}, bf16[128,512]{1,0:T(8,128)(2,1)}, u32[]{:S(2)}) copy-start(bf16[128,512]{1,0:T(8,128)(2,1)} %param.12) | copy-start | bytes 393220
  22.0 63.9 %all-to-all-start = ((bf16[128,1,64,256]{3,2,1,0:T(8,128)(2,1)}), bf16[128,1,64,256]{3,2,1,0:T(8,128)(2,1)}, u32[]{:S(2)}, u32[]{:S(2)}) async-start(bf16[128,1,64,256]{3,2,1,0:T(8,128)(2,1)} %bitcast.136), calls=%async_computation | async-start | bytes 8388608 | tf_op jit(solution)/shard_map/all_to_all | solution.py:60
  33.7 277.9 %all-reduce.2.cloned.1.call-start = ((), (), s32[]{:S(2)}) async-start(), calls=%async_computation.3 | async-start | bytes 16777216 | tf_op jit(solution)/shard_map/psum | solution.py:137
  119.1 0.7 copy-start.3
  119.1 405.7 %reduce-scatter.2.cloned.1.call-start = ((), (), s32[]{:S(2)}) async-start(), calls=%async_computation.4 | async-start | bytes 15335424 | tf_op jit(solution)/shard_map/reduce_scatter | solution.py:142
  365.2 167.2 %copy-start.1 = (bf16[512,2048]{1,0:T(8,128)(2,1)S(1)}, bf16[512,2048]{1,0:T(8,128)(2,1)}, u32[]{:S(2)}) copy-start(bf16[512,2048]{1,0:T(8,128)(2,1)} %param.19) | copy-start | bytes 6291460
Sparse Core Ops, SparseCore 0:
  119.2 192.2 all-reduce.1
  365.4 159.4 reduce-scatter.1
